TPU v7x, 32 devices: a whole 2x2x4 slice. The times are simulated.
32 devices in a mesh: groups: 2 (over y), tm: 4 (over z), space: 2 (over x), clip: 2 (over core).
Axes of the slice: x: 2, y: 2, z: 4, core: 2. Of those that a mesh axis runs over, the one named last changes fastest.
Arguments:
- features: bfloat16 [4, 16, 8, 16, 256], P(('groups', 'clip'), 'tm', 'space'), parts along dimension 0, may hold values from -6 to 6
- frame_counts: int32 [4], P(('groups', 'clip')), parts along dimension 0, may hold values from 1 to 16, as said below
- routes: int32 [4, 512, 1], P(('groups', 'clip'), ('tm', 'space')), parts along dimension 0, may hold values from 0 to 7; in each aligned block of 64 rows (0 to 63, 64 to 127, ..., all dimensions but the last counted through in order) at most 9 rows name the same one
- norm_gains: float32 [3, 256], replicated, may hold values from 0.5 to 1.5
- conv_weights: bfloat16 [2, 256, 27, 256], P(None, 'tm'), may hold values from -0.078125 to 0.078125
- conv_biases: float32 [2, 256], replicated, may hold values from -3 to 3
- latent_weight: bfloat16 [256, 16], replicated, may hold values from -0.375 to 0.375
- embed_weight: bfloat16 [64, 3072], replicated, may hold values from -0.75 to 0.75
- embed_bias: float32 [3072], replicated, may hold values from -3 to 3
Outputs:
- packed: bfloat16 [4, 576, 3072], P(('groups', 'clip'), ('tm', 'space')), parts along dimension 0
There are 2 independent parts, one for each index of `groups`. A program takes and returns all parts, laid end to end along the dimension named above; an argument that names none is the same for every part. Nothing has to cross between parts.
Inputs may be any that keep to these rules, and one draw needn't show every extreme that they name: `routes`: in each clip, the 64 patches of one span and tile name any one owner at most 9 times. `frame_counts`: one clip of each part has all 16 frames valid.
All inputs are finite; a program needn't handle non-finite values.
Results may differ from a plain program's by a relative error of at most 0.0054.
Values may be sent and summed in bfloat16 or wider, within the bound.
A program may use at most 64 MiB of HBM per device.

v0:
```python
import jax
import jax.numpy as jnp
from jax import lax
from jax.sharding import PartitionSpec as P


def shifted(block, axis, distance):
    devices = range(lax.axis_size(axis))
    route = [(i - distance, i) for i in devices if i - distance in devices]
    return lax.ppermute(block, axis, route)


def with_halo(cells, sides, width):
    for axis, dim in sides:
        count = lax.axis_size(axis)
        ends = count - 1
        head = lax.slice_in_dim(cells, 0, width, axis=dim)
        tail = lax.slice_in_dim(cells, cells.shape[dim] - width, cells.shape[dim], axis=dim)
        cells = jnp.concatenate(
            [
                lax.ppermute(tail, axis, [(i, (i + 1) % count) for i in range(ends)]),
                cells,
                lax.ppermute(head, axis, [((i + 1) % count, i) for i in range(ends)]),
            ],
            axis=dim,
        )
    return cells


def norm_silu(values, gain):
    scale = lax.rsqrt(jnp.mean(values * values, axis=-1, keepdims=True) + 1e-06)
    return jax.nn.silu(values * scale * gain)


def conv_taps(padded, weights):
    frames = padded.shape[0] - 2
    rows = padded.shape[1] - 2
    cols = padded.shape[2] - 2
    inner = padded.shape[3]
    outer = weights.shape[0]
    summed = jnp.zeros((frames * rows * cols, outer), jnp.float32)
    for frame_tap in range(3):
        columns = jnp.concatenate(
            [
                padded[
                    frame_tap : frame_tap + frames,
                    row_tap : row_tap + rows,
                    col_tap : col_tap + cols,
                ]
                for row_tap in range(3)
                for col_tap in range(3)
            ],
            axis=-1,
        )
        columns = columns.reshape(frames * rows * cols, 9 * inner)
        taps = weights[:, 9 * frame_tap : 9 * frame_tap + 9, :].reshape(outer, 9 * inner)
        summed = summed + lax.dot_general(
            columns, taps, (((1,), (1,)), ((), ())), preferred_element_type=jnp.float32
        )
    return summed.reshape(frames, rows, cols, outer)


def causal_layer(active, weights):
    earlier = shifted(active[-2:], "tm", 1)
    extended = jnp.concatenate([earlier, active], axis=0)
    rimmed = with_halo(extended, (("space", 1),), 1)
    padded = jnp.pad(rimmed, ((0, 0), (0, 0), (1, 1), (0, 0)))
    copies = lax.axis_size(("space", "clip"))
    share = weights.shape[2] // copies
    mine = lax.dynamic_slice_in_dim(weights, lax.axis_index(("space", "clip")) * share, share, 2)
    slices = lax.all_gather(mine, "tm", axis=0, tiled=True)
    return conv_taps(padded, lax.all_gather(slices, ("space", "clip"), axis=2, tiled=True))


def shards(
    features,
    frame_counts,
    routes,
    norm_gains,
    conv_weights,
    conv_biases,
    latent_weight,
    embed_weight,
    embed_bias,
):
    inputs = features[0].astype(jnp.float32)
    frames, rows, cols, width = inputs.shape
    active = norm_silu(inputs, norm_gains[0]).astype(jnp.bfloat16)
    hidden = causal_layer(active, conv_weights[0]) + conv_biases[0]
    active = norm_silu(hidden, norm_gains[1]).astype(jnp.bfloat16)
    hidden = causal_layer(active, conv_weights[1]) + conv_biases[1]
    merged = inputs + hidden
    active = norm_silu(merged, norm_gains[2]).astype(jnp.bfloat16)
    latent = jnp.dot(active.reshape(-1, width), latent_weight, preferred_element_type=jnp.float32)
    channels = latent_weight.shape[1]
    latent = latent.reshape(frames, rows // 2, 2, cols // 2, 2, channels)
    patches = latent.transpose(0, 1, 3, 2, 4, 5).reshape(-1, 4 * channels).astype(jnp.bfloat16)
    tok_count = patches.shape[0]
    owners = lax.axis_size("tm") * lax.axis_size("space")
    most_rows = (tok_count + owners - 1) // owners + 1
    destinations = routes[0, :, 0]
    positions = jnp.arange(tok_count, dtype=jnp.int32)
    before = positions[:, None] > positions[None, :]
    ranks = jnp.sum(
        ((destinations[:, None] == destinations[None, :]) & before).astype(jnp.int32), axis=1
    )
    targets = destinations * most_rows + ranks
    frame_ids = lax.axis_index("tm") * frames + positions // (rows // 2 * (cols // 2))
    alive = (frame_ids < frame_counts[0]).astype(jnp.bfloat16)
    placing = (jnp.arange(owners * most_rows, dtype=jnp.int32)[:, None] == targets[None, :]).astype(
        jnp.bfloat16
    )
    outgoing = jnp.dot(placing, patches, preferred_element_type=jnp.float32).astype(jnp.bfloat16)
    outgoing = outgoing.reshape(owners, most_rows, 4 * channels)
    marks = jnp.dot(placing, alive[:, None], preferred_element_type=jnp.float32).astype(
        jnp.bfloat16
    )
    marks = marks.reshape(owners, most_rows)
    tokens = lax.all_to_all(outgoing, ("tm", "space"), split_axis=0, concat_axis=0, tiled=True)
    flags = lax.all_to_all(marks, ("tm", "space"), split_axis=0, concat_axis=0, tiled=True)
    projected = (
        jnp.dot(
            tokens.reshape(-1, tokens.shape[2]), embed_weight, preferred_element_type=jnp.float32
        )
        + embed_bias
    )
    projected = projected * flags.reshape(-1, 1).astype(jnp.float32)
    packed_rows = projected.astype(jnp.bfloat16).reshape(tokens.shape[0], tokens.shape[1], -1)
    return packed_rows.reshape(1, -1, packed_rows.shape[2])


def solution(mesh):
    return jax.shard_map(
        shards,
        mesh=mesh,
        in_specs=(
            P(("groups", "clip"), "tm", "space", None, None),
            P(("groups", "clip")),
            P(("groups", "clip"), ("tm", "space"), None),
            P(),
            P(None, "tm", None, None),
            P(),
            P(),
            P(),
            P(),
        ),
        out_specs=P(("groups", "clip"), ("tm", "space"), None),
        check_vma=False,
    )
```

profile of v0, /device:TPU:0, one launch (start us, length us, event | category | flops | bytes accessed | tf_op | source)
XLA Modules:
  0.0 164.7 jit_solution(14299890801617923095)
XLA Ops:
  6.5 1.6 fusion.52
  8.1 0.2 constant_dynamic-slice_fusion.1
  8.3 0.3 copy.34
  8.6 39.7 %all-gather = bf16[1,256,27,64]{3,2,0,1:T(8,128)(2,1)S(1)} all-gather(bf16[1,64,27,64]{3,2,0,1:T(8,128)(2,1)S(1)} %copy.34), channel_id=2, replica_groups=mesh['groups'=2,'tm'=4,'space'=2,'clip'=2] {'tm'}, dimensions={1}, use_global_device_ids=true | all-gather | bytes 1105920 | tf_op jit(solution)/shard_map/all_gather | solution.py:71
  48.3 2.7 %copy.25 = bf16[1,256,27,64]{1,3,2,0:T(8,128)(2,1)} copy(bf16[1,256,27,64]{3,2,0,1:T(8,128)(2,1)S(1)} %all-gather) | data formatting | bytes 1769472 | tf_op jit(solution)/shard_map/all_gather | solution.py:71
  51.1 0.2 constant_dynamic-slice_fusion
  51.3 0.3 copy.36
  51.6 37.3 %all-gather.2 = bf16[1,256,27,64]{3,2,0,1:T(8,128)(2,1)S(1)} all-gather(bf16[1,64,27,64]{3,2,0,1:T(8,128)(2,1)S(1)} %copy.36), channel_id=4, replica_groups=mesh['groups'=2,'tm'=4,'space'=2,'clip'=2] {'tm'}, dimensions={1}, use_global_device_ids=true | all-gather | bytes 1105920 | tf_op jit(solution)/shard_map/all_gather | solution.py:71
  88.9 2.7 %copy.27 = bf16[1,256,27,64]{1,3,2,0:T(8,128)(2,1)} copy(bf16[1,256,27,64]{3,2,0,1:T(8,128)(2,1)S(1)} %all-gather.2) | data formatting | bytes 1769472 | tf_op jit(solution)/shard_map/all_gather | solution.py:71
  92.0 3.5 %collective-permute-start = (bf16[2,4,16,256]{3,2,1,0:T(8,128)(2,1)S(1)}, bf16[2,4,16,256]{3,2,1,0:T(8,128)(2,1)S(1)}, u32[]{:S(2)}, u32[]{:S(2)}) collective-permute-start(bf16[2,4,16,256]{3,2,1,0:T(8,128)(2,1)S(1)} %slice.322), channel_id=1, source_target_pairs={{0,4},{4,8},{8,12},{1,5},{5,9},{9,13},{2,6},{6,10},{10,14},{3,7},{... | collective-permute-start | bytes 196616 | tf_op jit(solution)/shard_map/ppermute | solution.py:10
  95.5 0.2 convert_reduce_fusion
  95.7 1.7 %collective-permute-done = bf16[2,4,16,256]{3,2,1,0:T(8,128)(2,1)S(1)} collective-permute-done((bf16[2,4,16,256]{3,2,1,0:T(8,128)(2,1)S(1)}, bf16[2,4,16,256]{3,2,1,0:T(8,128)(2,1)S(1)}, u32[]{:S(2)}, u32[]{:S(2)}) %collective-permute-start) | collective-permute-done | bytes 65568 | tf_op jit(solution)/shard_map/ppermute | solution.py:10
  97.4 3.4 %collective-permute-start.1 = (bf16[6,1,16,256]{3,2,1,0:T(8,128)(2,1)S(1)}, bf16[6,1,16,256]{3,2,1,0:T(8,128)(2,1)S(1)}, u32[]{:S(2)}, u32[]{:S(2)}) collective-permute-start(bf16[6,1,16,256]{3,2,1,0:T(8,128)(2,1)S(1)} %get-tuple-element.71), channel_id=1, source_target_pairs={{0,2},{1,3},{4,6},{5,7},{8,10},{9,11},{12,14},{13,15},{16,18},{17,... | collective-permute-start | bytes 147464 | tf_op jit(solution)/shard_map/ppermute | solution.py:21
  100.8 1.3 collective-permute-start.2
  102.8 0.6 collective-permute-done.1
  103.3 4.6 %collective-permute-done.2 = bf16[6,1,16,256]{3,2,1,0:T(8,128)(2,1)S(1)} collective-permute-done((bf16[6,1,16,256]{3,2,1,0:T(8,128)(2,1)S(1)}, bf16[6,1,16,256]{3,2,1,0:T(8,128)(2,1)S(1)}, u32[]{:S(2)}, u32[]{:S(2)}) %collective-permute-start.2) | collective-permute-done | bytes 49184 | tf_op jit(solution)/shard_map/ppermute | solution.py:23
  108.0 0.2 fusion.13
  108.3 0.8 slice_dynamic-update-slice_fusion.31
  109.1 0.8 slice_dynamic-update-slice_fusion.30
  109.8 0.8 slice_dynamic-update-slice_fusion.29
  110.6 0.8 slice_dynamic-update-slice_fusion.28
  111.4 0.8 fusion.27
  112.2 0.8 slice_dynamic-update-slice_fusion.27
  113.1 0.8 slice_dynamic-update-slice_fusion.26
  113.8 0.8 slice_dynamic-update-slice_fusion.25
  114.6 0.8 slice_dynamic-update-slice_fusion.24
  115.4 2.2 %fusion.51 = (bf16[256,9,256]{0,2,1:T(8,128)(2,1)S(1)}, bf16[256,9,256]{0,2,1:T(8,128)(2,1)S(1)}, bf16[256,9,256]{0,2,1:T(8,128)(2,1)S(1)}) fusion(bf16[256,27,256]{0,2,1:T(8,128)(2,1)} %bitcast.85), kind=kLoop, calls=%fused_computation.153 | loop fusion | bytes 7077888 | tf_op jit(solution)/shard_map/slice | solution.py:56
  117.6 1.7 %fusion.56 = f32[256,256]{1,0:T(8,128)S(1)} fusion(bf16[256,2304]{1,0:T(8,128)(2,1)} %bitcast.4, bf16[256,2304]{0,1:T(8,128)(2,1)S(1)} %bitcast.83), kind=kOutput, calls=%fused_computation.158 | convolution fusion | flops 301989888 | bytes 2621440 | tf_op jit(solution)/shard_map/dot_general | solution.py:57
  119.4 1.8 %convolution_add_fusion.4 = f32[256,256]{1,0:T(8,128)S(1)} fusion(f32[256,256]{1,0:T(8,128)S(1)} %fusion.56, bf16[256,2304]{1,0:T(8,128)(2,1)} %bitcast.7, bf16[256,2304]{0,1:T(8,128)(2,1)S(1)} %bitcast.82), kind=kOutput, calls=%fused_computation.9 | convolution fusion | flops 302055424 | bytes 2883584 | tf_op jit(solution)/shard_map/dot_general | solution.py:57
  121.1 0.6 multiply_reduce_fusion
  121.8 0.2 multiply_convert_fusion.1
  122.0 4.3 %collective-permute-start.3 = (bf16[2,4,16,256]{3,2,1,0:T(8,128)(2,1)S(1)}, bf16[2,4,16,256]{3,2,1,0:T(8,128)(2,1)S(1)}, u32[]{:S(2)}, u32[]{:S(2)}) collective-permute-start(bf16[2,4,16,256]{3,2,1,0:T(8,128)(2,1)S(1)} %slice.356), channel_id=1, source_target_pairs={{0,4},{4,8},{8,12},{1,5},{5,9},{9,13},{2,6},{6,10},{10,14},{3,7},{... | collective-permute-start | bytes 196616 | tf_op jit(solution)/shard_map/ppermute | solution.py:10
  126.4 0.7 all_to_all.12
  127.1 4.4 %all-to-all-start.1 = ((bf16[8,1,9]{2,1,0:T(2,128)(2,1)}), bf16[8,1,9]{2,1,0:T(2,128)(2,1)S(1)}, u32[]{:S(2)}, u32[]{:S(2)}) async-start(bf16[8,1,9]{2,1,0:T(2,128)(2,1)} %all_to_all.12), calls=%async_computation.1 | async-start | bytes 8192 | tf_op jit(solution)/shard_map/all_to_all | solution.py:120
  131.5 3.9 %collective-permute-start.4 = (bf16[6,1,16,256]{3,2,1,0:T(8,128)(2,1)S(1)}, bf16[6,1,16,256]{3,2,1,0:T(8,128)(2,1)S(1)}, u32[]{:S(2)}, u32[]{:S(2)}) collective-permute-start(bf16[6,1,16,256]{3,2,1,0:T(8,128)(2,1)S(1)} %get-tuple-element.65), channel_id=1, source_target_pairs={{0,2},{1,3},{4,6},{5,7},{8,10},{9,11},{12,14},{13,15},{16,18},{17,... | collective-permute-start | bytes 147464 | tf_op jit(solution)/shard_map/ppermute | solution.py:21
  135.4 1.3 collective-permute-start.5
  136.7 2.2 %fusion.50 = (bf16[256,9,256]{0,2,1:T(8,128)(2,1)S(1)}, bf16[256,9,256]{0,2,1:T(8,128)(2,1)S(1)}, bf16[256,9,256]{0,2,1:T(8,128)(2,1)S(1)}) fusion(bf16[256,27,256]{0,2,1:T(8,128)(2,1)} %bitcast.84), kind=kLoop, calls=%fused_computation.152 | loop fusion | bytes 7077888 | tf_op jit(solution)/shard_map/slice | solution.py:56
  139.0 2.4 %collective-permute-done.5 = bf16[6,1,16,256]{3,2,1,0:T(8,128)(2,1)S(1)} collective-permute-done((bf16[6,1,16,256]{3,2,1,0:T(8,128)(2,1)S(1)}, bf16[6,1,16,256]{3,2,1,0:T(8,128)(2,1)S(1)}, u32[]{:S(2)}, u32[]{:S(2)}) %collective-permute-start.5) | collective-permute-done | bytes 49184 | tf_op jit(solution)/shard_map/ppermute | solution.py:23
  141.4 0.2 select_maximum_fusion
  142.1 0.5 fusion.57
  142.6 0.5 convolution_add_fusion.2
  143.1 0.5 convolution_add_fusion.1
  144.1 0.2 copy-done.3
  144.6 0.2 convolution_convert_fusion.1
  144.9 0.7 reshape.170
  145.6 4.5 %all-to-all-start = ((bf16[8,2,288]{2,1,0:T(2,128)(2,1)}), bf16[8,2,288]{2,1,0:T(2,128)(2,1)S(1)}, u32[]{:S(2)}, u32[]{:S(2)}) async-start(bf16[8,2,288]{2,1,0:T(2,128)(2,1)} %reshape.170), calls=%async_computation | async-start | bytes 24576 | tf_op jit(solution)/shard_map/all_to_all | solution.py:119
  150.3 6.4 %all-to-all-done = bf16[8,2,288]{2,1,0:T(2,128)(2,1)S(1)} async-done(((bf16[8,2,288]{2,1,0:T(2,128)(2,1)}), bf16[8,2,288]{2,1,0:T(2,128)(2,1)S(1)}, u32[]{:S(2)}, u32[]{:S(2)}) %all-to-all-start) | async-done | bytes 9248 | tf_op jit(solution)/shard_map/all_to_all | solution.py:119
  156.9 1.0 fusion.2
  (60 shorter events, 2.3 us)
Async XLA Ops:
  6.5 150.3 %copy-start = (bf16[64,3072]{1,0:T(8,128)(2,1)S(1)}, bf16[64,3072]{1,0:T(8,128)(2,1)}, u32[]{:S(2)}) copy-start(bf16[64,3072]{1,0:T(8,128)(2,1)} %param.16) | copy-start | bytes 1179652
  6.5 108.9 %all-gather.7.cloned.1.call-start = ((), (), s32[]{:S(2)}) async-start(), calls=%async_computation.2 | async-start | bytes 4423680 | tf_op jit(solution)/shard_map/all_gather | solution.py:72
  51.1 85.7 %all-gather.9.cloned.1.call-start = ((), (), s32[]{:S(2)}) async-start(), calls=%async_computation.3 | async-start | bytes 4423680 | tf_op jit(solution)/shard_map/all_gather | solution.py:72
  88.9 2.7 %copy-start.1 = (bf16[1,4,4,16,256]{4,3,2,1,0:T(8,128)(2,1)S(1)}, bf16[1,4,4,16,256]{4,3,2,1,0:T(8,128)(2,1)}, u32[]{:S(2)}) copy-start(bf16[1,4,4,16,256]{4,3,2,1,0:T(8,128)(2,1)} %param.9) | copy-start | bytes 393220
  88.9 2.9 %copy-start.4 = (f32[3,256]{1,0:T(4,128)S(1)}, f32[3,256]{1,0:T(4,128)}, u32[]{:S(2)}) copy-start(f32[3,256]{1,0:T(4,128)} %param.12) | copy-start | bytes 9220
  91.6 3.9 %copy-start.5 = (f32[2,256]{1,0:T(2,128)S(1)}, f32[2,256]{1,0:T(2,128)}, u32[]{:S(2)}) copy-start(f32[2,256]{1,0:T(2,128)} %param.14) | copy-start | bytes 6148
  91.6 3.9 %copy-start.6 = (s32[1,64,1]{1,2,0:T(1,128)S(1)}, s32[1,64,1]{1,2,0:T(1,128)}, u32[]{:S(2)}) copy-start(s32[1,64,1]{1,2,0:T(1,128)} %param.11) | copy-start | bytes 772
  92.0 5.4 %collective-permute-start = (bf16[2,4,16,256]{3,2,1,0:T(8,128)(2,1)S(1)}, bf16[2,4,16,256]{3,2,1,0:T(8,128)(2,1)S(1)}, u32[]{:S(2)}, u32[]{:S(2)}) collective-permute-start(bf16[2,4,16,256]{3,2,1,0:T(8,128)(2,1)S(1)} %slice.322), channel_id=1, source_target_pairs={{0,4},{4,8},{8,12},{1,5},{5,9},{9,13},{2,6},{6,10},{10,14},{3,7},{... | collective-permute-start | bytes 196616 | tf_op jit(solution)/shard_map/ppermute | solution.py:10
  97.4 5.9 %collective-permute-start.1 = (bf16[6,1,16,256]{3,2,1,0:T(8,128)(2,1)S(1)}, bf16[6,1,16,256]{3,2,1,0:T(8,128)(2,1)S(1)}, u32[]{:S(2)}, u32[]{:S(2)}) collective-permute-start(bf16[6,1,16,256]{3,2,1,0:T(8,128)(2,1)S(1)} %get-tuple-element.71), channel_id=1, source_target_pairs={{0,2},{1,3},{4,6},{5,7},{8,10},{9,11},{12,14},{13,15},{16,18},{17,... | collective-permute-start | bytes 147464 | tf_op jit(solution)/shard_map/ppermute | solution.py:21
  100.8 7.2 %collective-permute-start.2 = (bf16[6,1,16,256]{3,2,1,0:T(8,128)(2,1)S(1)}, bf16[6,1,16,256]{3,2,1,0:T(8,128)(2,1)S(1)}, u32[]{:S(2)}, u32[]{:S(2)}) collective-permute-start(bf16[6,1,16,256]{3,2,1,0:T(8,128)(2,1)S(1)} %get-tuple-element.72), channel_id=1, source_target_pairs={{2,0},{3,1},{6,4},{7,5},{10,8},{11,9},{14,12},{15,13},{18,16},{19,... | collective-permute-start | bytes 147464 | tf_op jit(solution)/shard_map/ppermute | solution.py:23
  122.0 9.5 %collective-permute-start.3 = (bf16[2,4,16,256]{3,2,1,0:T(8,128)(2,1)S(1)}, bf16[2,4,16,256]{3,2,1,0:T(8,128)(2,1)S(1)}, u32[]{:S(2)}, u32[]{:S(2)}) collective-permute-start(bf16[2,4,16,256]{3,2,1,0:T(8,128)(2,1)S(1)} %slice.356), channel_id=1, source_target_pairs={{0,4},{4,8},{8,12},{1,5},{5,9},{9,13},{2,6},{6,10},{10,14},{3,7},{... | collective-permute-start | bytes 196616 | tf_op jit(solution)/shard_map/ppermute | solution.py:10
  127.1 18.6 %all-to-all-start.1 = ((bf16[8,1,9]{2,1,0:T(2,128)(2,1)}), bf16[8,1,9]{2,1,0:T(2,128)(2,1)S(1)}, u32[]{:S(2)}, u32[]{:S(2)}) async-start(bf16[8,1,9]{2,1,0:T(2,128)(2,1)} %all_to_all.12), calls=%async_computation.1 | async-start | bytes 8192 | tf_op jit(solution)/shard_map/all_to_all | solution.py:120
  131.5 7.5 %collective-permute-start.4 = (bf16[6,1,16,256]{3,2,1,0:T(8,128)(2,1)S(1)}, bf16[6,1,16,256]{3,2,1,0:T(8,128)(2,1)S(1)}, u32[]{:S(2)}, u32[]{:S(2)}) collective-permute-start(bf16[6,1,16,256]{3,2,1,0:T(8,128)(2,1)S(1)} %get-tuple-element.65), channel_id=1, source_target_pairs={{0,2},{1,3},{4,6},{5,7},{8,10},{9,11},{12,14},{13,15},{16,18},{17,... | collective-permute-start | bytes 147464 | tf_op jit(solution)/shard_map/ppermute | solution.py:21
  135.4 6.0 %collective-permute-start.5 = (bf16[6,1,16,256]{3,2,1,0:T(8,128)(2,1)S(1)}, bf16[6,1,16,256]{3,2,1,0:T(8,128)(2,1)S(1)}, u32[]{:S(2)}, u32[]{:S(2)}) collective-permute-start(bf16[6,1,16,256]{3,2,1,0:T(8,128)(2,1)S(1)} %get-tuple-element.66), channel_id=1, source_target_pairs={{2,0},{3,1},{6,4},{7,5},{10,8},{11,9},{14,12},{15,13},{18,16},{19,... | collective-permute-start | bytes 147464 | tf_op jit(solution)/shard_map/ppermute | solution.py:23
  143.6 0.7 copy-start.3
  143.6 13.3 %copy-start.2 = (f32[3072]{0:T(1024)S(1)}, f32[3072]{0:T(1024)}, u32[]{:S(2)}) copy-start(f32[3072]{0:T(1024)} %param.17) | copy-start | bytes 36868
  145.6 11.1 %all-to-all-start = ((bf16[8,2,288]{2,1,0:T(2,128)(2,1)}), bf16[8,2,288]{2,1,0:T(2,128)(2,1)S(1)}, u32[]{:S(2)}, u32[]{:S(2)}) async-start(bf16[8,2,288]{2,1,0:T(2,128)(2,1)} %reshape.170), calls=%async_computation | async-start | bytes 24576 | tf_op jit(solution)/shard_map/all_to_all | solution.py:119
Sparse Core Ops, SparseCore 0:
  51.2 32.3 all-gather.6
  91.8 33.0 all-gather.8
where the time goes:
time: 165 us
  blocking collectives  77 us (47%)
  starting transfers between devices  26.6 us (16%)
  local copies, waits for them, and re-layouts  21.5 us (13%)
  waiting for transfers between devices  15.8 us (10%)
  between operations  14.5 us (9%)
  matrix products  7 us (4%)
  other arithmetic  2.28 us (1%)
    all_gather x2, blocking collectives, causal_layer(): slices = lax.all_gather(mine, 'tm', axis=0, tiled=True)  77 us
    ppermute x2, starting transfers between devices, shifted(): return lax.ppermute(block, axis, route)  7.8 us
    unnamed x32, local copies, waits for them, and re-layouts  7.52 us
    ppermute x2, starting transfers between devices, with_halo(): lax.ppermute(tail, axis, [(i, (i + 1) % count) for i in range(ends)])  7.32 us
    ppermute x2, waiting for transfers between devices, with_halo(): lax.ppermute(head, axis, [((i + 1) % count, i) for i in range(ends)])  7.07 us
    all_to_all x1, waiting for transfers between devices, shards(): lax.all_to_all(outgoing, ('tm', 'space'), split_axis=0, concat_axis=0, ti...  6.45 us
    dot_general x6, matrix products, conv_taps(): lax.dot_general(columns, taps, (((1,), (1,)), ((), ())), preferred_elemen...  5.49 us
    all_gather x2, local copies, waits for them, and re-layouts, causal_layer(): slices = lax.all_gather(mine, 'tm', axis=0, tiled=True)  5.42 us
  transfers between devices with their start and end apart: 10, of which 5 were waited for; matrix products, arithmetic and copies ran while one was open for 15% of the time, Pallas kernels for 0%

commit v1 on v0

--- a/solution.py
+++ b/solution.py
@@ -68,7 +68,12 @@
     copies = lax.axis_size(("space", "clip"))
     share = weights.shape[2] // copies
     mine = lax.dynamic_slice_in_dim(weights, lax.axis_index(("space", "clip")) * share, share, 2)
-    slices = lax.all_gather(mine, "tm", axis=0, tiled=True)
+    ring = [mine]
+    for hop in range(3):
+        ring.append(lax.ppermute(ring[-1], "tm", [(dev, (dev + 1) % 4) for dev in range(4)]))
+    slices = jnp.roll(
+        jnp.concatenate(ring[::-1], axis=0), (lax.axis_index("tm") + 1) * ring[0].shape[0], axis=0
+    )
     return conv_taps(padded, lax.all_gather(slices, ("space", "clip"), axis=2, tiled=True))
 
 

time: 165 us -> 160 us (0.970)
  blocking collectives: 77 us -> 0 us
  waiting for transfers between devices: 15.8 us -> 85.2 us
  other arithmetic: 2.28 us -> 12.7 us
  local copies, waits for them, and re-layouts: 21.5 us -> 15.4 us
    all_gather x2 -> x0, blocking collectives: 77 us -> none  [causal_layer(): slices = lax.all_gather(mine, 'tm', axis=0, tiled=True)]
    ppermute x0 -> x6, waiting for transfers between devices: none -> 69.5 us  [causal_layer(): lax.ppermute(ring[-1], 'tm', [(dev, (dev + 1) % 4) for dev in range(4)])]
    concatenate x0 -> x2, other arithmetic: none -> 10.5 us  [causal_layer(): jnp.roll(jnp.concatenate(ring[::-1], axis=0), (lax.axis_index('tm') + 1)...]
    all_gather x2 -> x0, local copies, waits for them, and re-layouts: 5.42 us -> none  [causal_layer(): slices = lax.all_gather(mine, 'tm', axis=0, tiled=True)]
    ppermute x0 -> x6, starting transfers between devices: none -> 3.17 us  [causal_layer(): lax.ppermute(ring[-1], 'tm', [(dev, (dev + 1) % 4) for dev in range(4)])]
    ppermute x2, starting transfers between devices: 7.8 us -> 5.6 us  [shifted(): return lax.ppermute(block, axis, route)]
    unnamed x32 -> x30, local copies, waits for them, and re-layouts: 7.52 us -> 6.38 us
  transfers between devices with their start and end apart: 10 -> 16, of which waited for: 5 -> 11; matrix products, arithmetic and copies ran while one was open for 15% -> 15% of each run, Pallas kernels for 0% -> 0%
where the time goes in v1:
time: 160 us; the launch traced here: 159 us
  waiting for transfers between devices  85.2 us (53%)
  starting transfers between devices  25.7 us (16%)
  local copies, waits for them, and re-layouts  15.4 us (10%)
  between operations  14.5 us (9%)
  other arithmetic  12.7 us (8%)
  matrix products  5.72 us (4%)
    ppermute x6, waiting for transfers between devices, causal_layer(): lax.ppermute(ring[-1], 'tm', [(dev, (dev + 1) % 4) for dev in range(4)])  69.5 us
    concatenate x2, other arithmetic, causal_layer(): jnp.roll(jnp.concatenate(ring[::-1], axis=0), (lax.axis_index('tm') + 1)...  10.5 us
    ppermute x2, waiting for transfers between devices, with_halo(): lax.ppermute(head, axis, [((i + 1) % count, i) for i in range(ends)])  6.92 us
    all_to_all x1, waiting for transfers between devices, shards(): lax.all_to_all(outgoing, ('tm', 'space'), split_axis=0, concat_axis=0, ti...  6.45 us
    unnamed x30, local copies, waits for them, and re-layouts  6.38 us
    ppermute x2, starting transfers between devices, with_halo(): lax.ppermute(tail, axis, [(i, (i + 1) % count) for i in range(ends)])  6.33 us
    ppermute x2, starting transfers between devices, shifted(): return lax.ppermute(block, axis, route)  5.6 us
    all_to_all x1, starting transfers between devices, shards(): lax.all_to_all(outgoing, ('tm', 'space'), split_axis=0, concat_axis=0, ti...  4.58 us
  transfers between devices with their start and end apart: 16, of which 11 were waited for; matrix products, arithmetic and copies ran while one was open for 15% of the time, Pallas kernels for 0%

profile of v1, /device:TPU:0, one launch (start us, length us, event | category | flops | bytes accessed | tf_op | source)
XLA Modules:
  0.0 159.2 jit_solution(4425635512948171180)
XLA Ops:
  6.5 1.6 %fusion.66 = (bf16[1,64,27,256]{3,1,2,0:T(8,128)(2,1)S(1)}, bf16[1,64,27,256]{3,1,2,0:T(8,128)(2,1)S(1)}) fusion(bf16[2,64,27,256]{3,1,2,0:T(8,128)(2,1)} %param.15), kind=kLoop, calls=%fused_computation.184 | loop fusion | bytes 3538944 | tf_op jit(solution)/shard_map/slice | solution.py:96
  8.1 0.3 constant_dynamic-slice_fusion
  8.5 0.2 copy.22
  8.7 3.1 %collective-permute-start.3 = (bf16[64,27,64]{0,2,1:T(8,128)(2,1)S(1)}, bf16[64,27,64]{0,2,1:T(8,128)(2,1)S(1)}, u32[]{:S(2)}, u32[]{:S(2)}) collective-permute-start(bf16[64,27,64]{0,2,1:T(8,128)(2,1)S(1)} %bitcast.85), channel_id=1, source_target_pairs={{0,4},{4,8},{8,12},{12,0},{1,5},{5,9},{9,13},{13,1},{2,6},{6,10},{... | collective-permute-start | bytes 663560 | tf_op jit(solution)/shard_map/ppermute | solution.py:73
  11.8 12.2 %collective-permute-done.3 = bf16[64,27,64]{0,2,1:T(8,128)(2,1)S(1)} collective-permute-done((bf16[64,27,64]{0,2,1:T(8,128)(2,1)S(1)}, bf16[64,27,64]{0,2,1:T(8,128)(2,1)S(1)}, u32[]{:S(2)}, u32[]{:S(2)}) %collective-permute-start.3) | collective-permute-done | bytes 221216 | tf_op jit(solution)/shard_map/ppermute | solution.py:73
  24.0 13.1 %collective-permute-done.4 = bf16[64,27,64]{0,2,1:T(8,128)(2,1)S(1)} collective-permute-done((bf16[64,27,64]{0,2,1:T(8,128)(2,1)S(1)}, bf16[64,27,64]{0,2,1:T(8,128)(2,1)S(1)}, u32[]{:S(2)}, u32[]{:S(2)}) %collective-permute-start.4) | collective-permute-done | bytes 221216 | tf_op jit(solution)/shard_map/ppermute | solution.py:73
  37.2 12.3 %collective-permute-done.5 = bf16[64,27,64]{0,2,1:T(8,128)(2,1)S(1)} collective-permute-done((bf16[64,27,64]{0,2,1:T(8,128)(2,1)S(1)}, bf16[64,27,64]{0,2,1:T(8,128)(2,1)S(1)}, u32[]{:S(2)}, u32[]{:S(2)}) %collective-permute-start.5) | collective-permute-done | bytes 221216 | tf_op jit(solution)/shard_map/ppermute | solution.py:73
  49.4 5.2 %fusion.15 = bf16[256,27,64]{0,2,1:T(8,128)(2,1)} fusion(s32[]{:T(128)S(6)} %select_n.26, bf16[64,27,64]{0,2,1:T(8,128)(2,1)S(1)} %collective-permute-done.5, bf16[64,27,64]{0,2,1:T(8,128)(2,1)S(1)} %collective-permute-done.4, bf16[64,27,64]{0,2,1:T(8,128)(2,1)S(1)} %collective-permute-done.3, bf16[64,27,64]{0,2,1:T(8,128)(2,1)S(1)} %bitcast.86), kind=kLoop, calls=%fused_computation.41 | loop fusion | flops 7077888 | bytes 1769476 | tf_op jit(solution)/shard_map/jit(_roll_dynamic)/concatenate | solution.py:74
  54.7 0.2 copy.23
  55.1 11.4 %collective-permute-done.9 = bf16[64,27,64]{0,2,1:T(8,128)(2,1)S(1)} collective-permute-done((bf16[64,27,64]{0,2,1:T(8,128)(2,1)S(1)}, bf16[64,27,64]{0,2,1:T(8,128)(2,1)S(1)}, u32[]{:S(2)}, u32[]{:S(2)}) %collective-permute-start.9) | collective-permute-done | bytes 221216 | tf_op jit(solution)/shard_map/ppermute | solution.py:73
  66.6 10.4 %collective-permute-done.10 = bf16[64,27,64]{0,2,1:T(8,128)(2,1)S(1)} collective-permute-done((bf16[64,27,64]{0,2,1:T(8,128)(2,1)S(1)}, bf16[64,27,64]{0,2,1:T(8,128)(2,1)S(1)}, u32[]{:S(2)}, u32[]{:S(2)}) %collective-permute-start.10) | collective-permute-done | bytes 221216 | tf_op jit(solution)/shard_map/ppermute | solution.py:73
  77.1 10.1 %collective-permute-done.11 = bf16[64,27,64]{0,2,1:T(8,128)(2,1)S(1)} collective-permute-done((bf16[64,27,64]{0,2,1:T(8,128)(2,1)S(1)}, bf16[64,27,64]{0,2,1:T(8,128)(2,1)S(1)}, u32[]{:S(2)}, u32[]{:S(2)}) %collective-permute-start.11) | collective-permute-done | bytes 221216 | tf_op jit(solution)/shard_map/ppermute | solution.py:73
  87.1 5.3 %fusion.8 = bf16[256,27,64]{0,2,1:T(8,128)(2,1)} fusion(s32[]{:T(128)S(6)} %select_n.26, bf16[64,27,64]{0,2,1:T(8,128)(2,1)S(1)} %collective-permute-done.11, bf16[64,27,64]{0,2,1:T(8,128)(2,1)S(1)} %collective-permute-done.10, bf16[64,27,64]{0,2,1:T(8,128)(2,1)S(1)} %collective-permute-done.9, bf16[64,27,64]{0,2,1:T(8,128)(2,1)S(1)} %bitcast.88), kind=kLoop, calls=%fused_computation.34 | loop fusion | flops 7077888 | bytes 1769476 | tf_op jit(solution)/shard_map/jit(_roll_dynamic)/concatenate | solution.py:74
  92.6 1.3 collective-permute-start
  94.1 1.7 %collective-permute-done = bf16[2,4,16,256]{3,2,1,0:T(8,128)(2,1)S(1)} collective-permute-done((bf16[2,4,16,256]{3,2,1,0:T(8,128)(2,1)S(1)}, bf16[2,4,16,256]{3,2,1,0:T(8,128)(2,1)S(1)}, u32[]{:S(2)}, u32[]{:S(2)}) %collective-permute-start) | collective-permute-done | bytes 65568 | tf_op jit(solution)/shard_map/ppermute | solution.py:10
  95.8 2.5 %collective-permute-start.1 = (bf16[6,1,16,256]{3,2,1,0:T(8,128)(2,1)S(1)}, bf16[6,1,16,256]{3,2,1,0:T(8,128)(2,1)S(1)}, u32[]{:S(2)}, u32[]{:S(2)}) collective-permute-start(bf16[6,1,16,256]{3,2,1,0:T(8,128)(2,1)S(1)} %get-tuple-element.72), channel_id=1, source_target_pairs={{0,2},{1,3},{4,6},{5,7},{8,10},{9,11},{12,14},{13,15},{16,18},{17,... | collective-permute-start | bytes 147464 | tf_op jit(solution)/shard_map/ppermute | solution.py:21
  98.4 1.5 collective-permute-start.2
  100.5 0.5 collective-permute-done.1
  101.0 4.5 %collective-permute-done.2 = bf16[6,1,16,256]{3,2,1,0:T(8,128)(2,1)S(1)} collective-permute-done((bf16[6,1,16,256]{3,2,1,0:T(8,128)(2,1)S(1)}, bf16[6,1,16,256]{3,2,1,0:T(8,128)(2,1)S(1)}, u32[]{:S(2)}, u32[]{:S(2)}) %collective-permute-start.2) | collective-permute-done | bytes 49184 | tf_op jit(solution)/shard_map/ppermute | solution.py:23
  105.5 0.2 fusion.27
  105.8 0.7 slice_dynamic-update-slice_fusion.31
  106.5 0.7 slice_dynamic-update-slice_fusion.30
  107.2 0.8 slice_dynamic-update-slice_fusion.29
  108.0 0.7 slice_dynamic-update-slice_fusion.28
  108.7 0.7 fusion.41
  109.4 0.7 slice_dynamic-update-slice_fusion.27
  110.1 0.7 slice_dynamic-update-slice_fusion.26
  110.9 0.7 slice_dynamic-update-slice_fusion.25
  111.5 0.7 slice_dynamic-update-slice_fusion.24
  112.3 2.2 %fusion.65 = (bf16[256,9,256]{0,2,1:T(8,128)(2,1)S(1)}, bf16[256,9,256]{0,2,1:T(8,128)(2,1)S(1)}, bf16[256,9,256]{0,2,1:T(8,128)(2,1)S(1)}) fusion(bf16[256,27,256]{0,2,1:T(8,128)(2,1)} %all-gather.3.cloned.1.call-done), kind=kLoop, calls=%fused_computation.183 | loop fusion | bytes 7077888 | tf_op jit(solution)/shard_map/slice | solution.py:56
  114.5 1.7 %fusion.70 = f32[256,256]{1,0:T(8,128)S(1)} fusion(bf16[256,2304]{1,0:T(8,128)(2,1)} %bitcast.4, bf16[256,2304]{0,1:T(8,128)(2,1)S(1)} %bitcast.83), kind=kOutput, calls=%fused_computation.188 | convolution fusion | flops 301989888 | bytes 2621440 | tf_op jit(solution)/shard_map/dot_general | solution.py:57
  116.3 0.5 convolution_add_fusion.4
  116.8 0.6 multiply_reduce_fusion
  117.6 4.3 %collective-permute-start.6 = (bf16[2,4,16,256]{3,2,1,0:T(8,128)(2,1)S(1)}, bf16[2,4,16,256]{3,2,1,0:T(8,128)(2,1)S(1)}, u32[]{:S(2)}, u32[]{:S(2)}) collective-permute-start(bf16[2,4,16,256]{3,2,1,0:T(8,128)(2,1)S(1)} %slice.356), channel_id=1, source_target_pairs={{0,4},{4,8},{8,12},{1,5},{5,9},{9,13},{2,6},{6,10},{10,14},{3,7},{... | collective-permute-start | bytes 196616 | tf_op jit(solution)/shard_map/ppermute | solution.py:10
  122.1 0.7 all_to_all.12
  122.7 3.2 %all-to-all-start.1 = ((bf16[8,1,9]{2,1,0:T(2,128)(2,1)}), bf16[8,1,9]{2,1,0:T(2,128)(2,1)S(1)}, u32[]{:S(2)}, u32[]{:S(2)}) async-start(bf16[8,1,9]{2,1,0:T(2,128)(2,1)} %all_to_all.12), calls=%async_computation.1 | async-start | bytes 8192 | tf_op jit(solution)/shard_map/all_to_all | solution.py:125
  126.0 3.8 %collective-permute-start.7 = (bf16[6,1,16,256]{3,2,1,0:T(8,128)(2,1)S(1)}, bf16[6,1,16,256]{3,2,1,0:T(8,128)(2,1)S(1)}, u32[]{:S(2)}, u32[]{:S(2)}) collective-permute-start(bf16[6,1,16,256]{3,2,1,0:T(8,128)(2,1)S(1)} %get-tuple-element.66), channel_id=1, source_target_pairs={{0,2},{1,3},{4,6},{5,7},{8,10},{9,11},{12,14},{13,15},{16,18},{17,... | collective-permute-start | bytes 147464 | tf_op jit(solution)/shard_map/ppermute | solution.py:21
  129.9 1.3 collective-permute-start.8
  131.2 2.2 %fusion.64 = (bf16[256,9,256]{0,2,1:T(8,128)(2,1)S(1)}, bf16[256,9,256]{0,2,1:T(8,128)(2,1)S(1)}, bf16[256,9,256]{0,2,1:T(8,128)(2,1)S(1)}) fusion(bf16[256,27,256]{0,2,1:T(8,128)(2,1)} %all-gather.5.cloned.1.call-done), kind=kLoop, calls=%fused_computation.182 | loop fusion | bytes 7077888 | tf_op jit(solution)/shard_map/slice | solution.py:56
  133.4 2.4 %collective-permute-done.8 = bf16[6,1,16,256]{3,2,1,0:T(8,128)(2,1)S(1)} collective-permute-done((bf16[6,1,16,256]{3,2,1,0:T(8,128)(2,1)S(1)}, bf16[6,1,16,256]{3,2,1,0:T(8,128)(2,1)S(1)}, u32[]{:S(2)}, u32[]{:S(2)}) %collective-permute-start.8) | collective-permute-done | bytes 49184 | tf_op jit(solution)/shard_map/ppermute | solution.py:23
  135.8 0.2 select_maximum_fusion
  136.6 0.5 fusion.71
  137.1 0.5 convolution_add_fusion.2
  137.5 0.5 convolution_add_fusion.1
  139.4 0.7 reshape.166
  140.1 4.6 %all-to-all-start = ((bf16[8,2,288]{2,1,0:T(2,128)(2,1)}), bf16[8,2,288]{2,1,0:T(2,128)(2,1)S(1)}, u32[]{:S(2)}, u32[]{:S(2)}) async-start(bf16[8,2,288]{2,1,0:T(2,128)(2,1)} %reshape.166), calls=%async_computation | async-start | bytes 24576 | tf_op jit(solution)/shard_map/all_to_all | solution.py:124
  144.8 6.4 %all-to-all-done = bf16[8,2,288]{2,1,0:T(2,128)(2,1)S(1)} async-done(((bf16[8,2,288]{2,1,0:T(2,128)(2,1)}), bf16[8,2,288]{2,1,0:T(2,128)(2,1)S(1)}, u32[]{:S(2)}, u32[]{:S(2)}) %all-to-all-start) | async-done | bytes 9248 | tf_op jit(solution)/shard_map/all_to_all | solution.py:124
  151.4 1.0 fusion.2
  (69 shorter events, 3.1 us)
Async XLA Ops:
  6.5 144.8 %copy-start = (bf16[64,3072]{1,0:T(8,128)(2,1)S(1)}, bf16[64,3072]{1,0:T(8,128)(2,1)}, u32[]{:S(2)}) copy-start(bf16[64,3072]{1,0:T(8,128)(2,1)} %param.18) | copy-start | bytes 1179652
  6.5 105.7 %all-gather.3.cloned.1.call-start = ((), (), s32[]{:S(2)}) async-start(), calls=%async_computation.2 | async-start | bytes 4423680 | tf_op jit(solution)/shard_map/all_gather | solution.py:77
  8.7 15.3 %collective-permute-start.3 = (bf16[64,27,64]{0,2,1:T(8,128)(2,1)S(1)}, bf16[64,27,64]{0,2,1:T(8,128)(2,1)S(1)}, u32[]{:S(2)}, u32[]{:S(2)}) collective-permute-start(bf16[64,27,64]{0,2,1:T(8,128)(2,1)S(1)} %bitcast.85), channel_id=1, source_target_pairs={{0,4},{4,8},{8,12},{12,0},{1,5},{5,9},{9,13},{13,1},{2,6},{6,10},{... | collective-permute-start | bytes 663560 | tf_op jit(solution)/shard_map/ppermute | solution.py:73
  24.0 13.1 %collective-permute-start.4 = (bf16[64,27,64]{0,2,1:T(8,128)(2,1)S(1)}, bf16[64,27,64]{0,2,1:T(8,128)(2,1)S(1)}, u32[]{:S(2)}, u32[]{:S(2)}) collective-permute-start(bf16[64,27,64]{0,2,1:T(8,128)(2,1)S(1)} %collective-permute-done.3), channel_id=1, source_target_pairs={{0,4},{4,8},{8,12},{12,0},{1,5},{5,9},{9,13},{13,1},{2,6},{6,10},{... | collective-permute-start | bytes 663560 | tf_op jit(solution)/shard_map/ppermute | solution.py:73
  37.2 12.3 %collective-permute-start.5 = (bf16[64,27,64]{0,2,1:T(8,128)(2,1)S(1)}, bf16[64,27,64]{0,2,1:T(8,128)(2,1)S(1)}, u32[]{:S(2)}, u32[]{:S(2)}) collective-permute-start(bf16[64,27,64]{0,2,1:T(8,128)(2,1)S(1)} %collective-permute-done.4), channel_id=1, source_target_pairs={{0,4},{4,8},{8,12},{12,0},{1,5},{5,9},{9,13},{13,1},{2,6},{6,10},{... | collective-permute-start | bytes 663560 | tf_op jit(solution)/shard_map/ppermute | solution.py:73
  54.7 11.8 %copy-start.1 = (bf16[1,4,4,16,256]{4,3,2,1,0:T(8,128)(2,1)S(1)}, bf16[1,4,4,16,256]{4,3,2,1,0:T(8,128)(2,1)}, u32[]{:S(2)}) copy-start(bf16[1,4,4,16,256]{4,3,2,1,0:T(8,128)(2,1)} %param.11) | copy-start | bytes 393220
  54.7 76.5 %all-gather.5.cloned.1.call-start = ((), (), s32[]{:S(2)}) async-start(), calls=%async_computation.3 | async-start | bytes 4423680 | tf_op jit(solution)/shard_map/all_gather | solution.py:77
  55.0 11.5 %collective-permute-start.9 = (bf16[64,27,64]{0,2,1:T(8,128)(2,1)S(1)}, bf16[64,27,64]{0,2,1:T(8,128)(2,1)S(1)}, u32[]{:S(2)}, u32[]{:S(2)}) collective-permute-start(bf16[64,27,64]{0,2,1:T(8,128)(2,1)S(1)} %bitcast.87), channel_id=1, source_target_pairs={{0,4},{4,8},{8,12},{12,0},{1,5},{5,9},{9,13},{13,1},{2,6},{6,10},{... | collective-permute-start | bytes 663560 | tf_op jit(solution)/shard_map/ppermute | solution.py:73
  66.5 10.6 %collective-permute-start.10 = (bf16[64,27,64]{0,2,1:T(8,128)(2,1)S(1)}, bf16[64,27,64]{0,2,1:T(8,128)(2,1)S(1)}, u32[]{:S(2)}, u32[]{:S(2)}) collective-permute-start(bf16[64,27,64]{0,2,1:T(8,128)(2,1)S(1)} %collective-permute-done.9), channel_id=1, source_target_pairs={{0,4},{4,8},{8,12},{12,0},{1,5},{5,9},{9,13},{13,1},{2,6},{6,10},{... | collective-permute-start | bytes 663560 | tf_op jit(solution)/shard_map/ppermute | solution.py:73
  77.0 10.1 %collective-permute-start.11 = (bf16[64,27,64]{0,2,1:T(8,128)(2,1)S(1)}, bf16[64,27,64]{0,2,1:T(8,128)(2,1)S(1)}, u32[]{:S(2)}, u32[]{:S(2)}) collective-permute-start(bf16[64,27,64]{0,2,1:T(8,128)(2,1)S(1)} %collective-permute-done.10), channel_id=1, source_target_pairs={{0,4},{4,8},{8,12},{12,0},{1,5},{5,9},{9,13},{13,1},{2,6},{6,10},{... | collective-permute-start | bytes 663560 | tf_op jit(solution)/shard_map/ppermute | solution.py:73
  77.0 15.4 %copy-start.4 = (f32[3,256]{1,0:T(4,128)S(1)}, f32[3,256]{1,0:T(4,128)}, u32[]{:S(2)}) copy-start(f32[3,256]{1,0:T(4,128)} %param.14) | copy-start | bytes 9220
  92.4 1.5 copy-start.5
  92.4 1.5 copy-start.6
  92.6 3.2 %collective-permute-start = (bf16[2,4,16,256]{3,2,1,0:T(8,128)(2,1)S(1)}, bf16[2,4,16,256]{3,2,1,0:T(8,128)(2,1)S(1)}, u32[]{:S(2)}, u32[]{:S(2)}) collective-permute-start(bf16[2,4,16,256]{3,2,1,0:T(8,128)(2,1)S(1)} %slice.322), channel_id=1, source_target_pairs={{0,4},{4,8},{8,12},{1,5},{5,9},{9,13},{2,6},{6,10},{10,14},{3,7},{... | collective-permute-start | bytes 196616 | tf_op jit(solution)/shard_map/ppermute | solution.py:10
  95.8 5.2 %collective-permute-start.1 = (bf16[6,1,16,256]{3,2,1,0:T(8,128)(2,1)S(1)}, bf16[6,1,16,256]{3,2,1,0:T(8,128)(2,1)S(1)}, u32[]{:S(2)}, u32[]{:S(2)}) collective-permute-start(bf16[6,1,16,256]{3,2,1,0:T(8,128)(2,1)S(1)} %get-tuple-element.72), channel_id=1, source_target_pairs={{0,2},{1,3},{4,6},{5,7},{8,10},{9,11},{12,14},{13,15},{16,18},{17,... | collective-permute-start | bytes 147464 | tf_op jit(solution)/shard_map/ppermute | solution.py:21
  98.4 7.2 %collective-permute-start.2 = (bf16[6,1,16,256]{3,2,1,0:T(8,128)(2,1)S(1)}, bf16[6,1,16,256]{3,2,1,0:T(8,128)(2,1)S(1)}, u32[]{:S(2)}, u32[]{:S(2)}) collective-permute-start(bf16[6,1,16,256]{3,2,1,0:T(8,128)(2,1)S(1)} %get-tuple-element.73), channel_id=1, source_target_pairs={{2,0},{3,1},{6,4},{7,5},{10,8},{11,9},{14,12},{15,13},{18,16},{19,... | collective-permute-start | bytes 147464 | tf_op jit(solution)/shard_map/ppermute | solution.py:23
  117.6 8.4 %collective-permute-start.6 = (bf16[2,4,16,256]{3,2,1,0:T(8,128)(2,1)S(1)}, bf16[2,4,16,256]{3,2,1,0:T(8,128)(2,1)S(1)}, u32[]{:S(2)}, u32[]{:S(2)}) collective-permute-start(bf16[2,4,16,256]{3,2,1,0:T(8,128)(2,1)S(1)} %slice.356), channel_id=1, source_target_pairs={{0,4},{4,8},{8,12},{1,5},{5,9},{9,13},{2,6},{6,10},{10,14},{3,7},{... | collective-permute-start | bytes 196616 | tf_op jit(solution)/shard_map/ppermute | solution.py:10
  122.7 17.3 %all-to-all-start.1 = ((bf16[8,1,9]{2,1,0:T(2,128)(2,1)}), bf16[8,1,9]{2,1,0:T(2,128)(2,1)S(1)}, u32[]{:S(2)}, u32[]{:S(2)}) async-start(bf16[8,1,9]{2,1,0:T(2,128)(2,1)} %all_to_all.12), calls=%async_computation.1 | async-start | bytes 8192 | tf_op jit(solution)/shard_map/all_to_all | solution.py:125
  126.0 7.4 %collective-permute-start.7 = (bf16[6,1,16,256]{3,2,1,0:T(8,128)(2,1)S(1)}, bf16[6,1,16,256]{3,2,1,0:T(8,128)(2,1)S(1)}, u32[]{:S(2)}, u32[]{:S(2)}) collective-permute-start(bf16[6,1,16,256]{3,2,1,0:T(8,128)(2,1)S(1)} %get-tuple-element.66), channel_id=1, source_target_pairs={{0,2},{1,3},{4,6},{5,7},{8,10},{9,11},{12,14},{13,15},{16,18},{17,... | collective-permute-start | bytes 147464 | tf_op jit(solution)/shard_map/ppermute | solution.py:21
  129.9 6.0 %collective-permute-start.8 = (bf16[6,1,16,256]{3,2,1,0:T(8,128)(2,1)S(1)}, bf16[6,1,16,256]{3,2,1,0:T(8,128)(2,1)S(1)}, u32[]{:S(2)}, u32[]{:S(2)}) collective-permute-start(bf16[6,1,16,256]{3,2,1,0:T(8,128)(2,1)S(1)} %get-tuple-element.67), channel_id=1, source_target_pairs={{2,0},{3,1},{6,4},{7,5},{10,8},{11,9},{14,12},{15,13},{18,16},{19,... | collective-permute-start | bytes 147464 | tf_op jit(solution)/shard_map/ppermute | solution.py:23
  138.0 0.7 copy-start.3
  138.0 13.3 %copy-start.2 = (f32[3072]{0:T(1024)S(1)}, f32[3072]{0:T(1024)}, u32[]{:S(2)}) copy-start(f32[3072]{0:T(1024)} %param.19) | copy-start | bytes 36868
  140.1 11.1 %all-to-all-start = ((bf16[8,2,288]{2,1,0:T(2,128)(2,1)}), bf16[8,2,288]{2,1,0:T(2,128)(2,1)S(1)}, u32[]{:S(2)}, u32[]{:S(2)}) async-start(bf16[8,2,288]{2,1,0:T(2,128)(2,1)} %reshape.166), calls=%async_computation | async-start | bytes 24576 | tf_op jit(solution)/shard_map/all_to_all | solution.py:124
Sparse Core Ops, SparseCore 0:
  54.8 28.4 all-gather.2
  92.6 28.5 all-gather.4
